TPU v7x, 128 devices: a whole 4x4x4 slice. The times are simulated.
128 devices in a mesh: rows: 64 (over y, z, x), cols: 2 (over core).
Axes of the slice: x: 4, y: 4, z: 4, core: 2. Of those that a mesh axis runs over, the one named last changes fastest.
Arguments:
- video: bfloat16 [512, 256, 256], P('rows', 'cols'), may hold values from -12 to 12
- foreground: float32 [512, 256, 256], P('rows', 'cols'), may hold values from -4 to 4
- scaled_dual: float32 [512, 256, 256], P('rows', 'cols'), may hold values from -2.5 to 2.5
Outputs:
- background: float32 [512, 256, 256], P('rows', 'cols')
- new_foreground: float32 [512, 256, 256], P('rows', 'cols')
- new_dual: float32 [512, 256, 256], P('rows', 'cols')
All inputs are finite; a program needn't handle non-finite values.
Results may differ from a plain program's by a relative error of at most 0.00035.
Values sent between devices are 32-bit elements; how exact they have to be, the bound alone decides.
A program may use at most 64 MiB of HBM per device.

v0:
```python
import jax
import jax.numpy as jnp
from jax import lax
from jax.sharding import PartitionSpec as P

K_ROOT = 8
K_SIGN = 6
K_TV = 8
threshold_ratio = 1.0
dual_step = 0.25
tv_weight = 1.0
HALO = K_TV


def shifted(x, axis, by):
    length = lax.axis_size(axis)
    pairs = [(i, i + by) for i in range(length) if 0 <= i + by < length]
    return lax.ppermute(x, axis, pairs)


def matmul(left, right):
    return jnp.dot(left, right, precision=lax.Precision.HIGHEST, preferred_element_type=jnp.float32)


def shrink_matrix(gram):
    size = gram.shape[0]
    identity = jnp.eye(size, dtype=jnp.float32)
    scale = jnp.sqrt(jnp.sum(gram * gram))
    root = gram / scale
    inverse = identity
    for sweep in range(K_ROOT):
        factor = 1.5 * identity - 0.5 * matmul(inverse, root)
        root = matmul(root, factor)
        inverse = matmul(factor, inverse)
    cutoff = threshold_ratio * jnp.trace(root) / size
    signed = root - cutoff * identity
    for sweep in range(K_SIGN):
        signed = 1.5 * signed - 0.5 * matmul(signed, matmul(signed, signed))
    return 0.5 * matmul(identity - cutoff * inverse, identity + signed)


def with_halo(pair):
    left = shifted(pair[:, :, -HALO:], "cols", 1)
    right = shifted(pair[:, :, :HALO], "cols", -1)
    pair = jnp.concatenate([left, pair, right], axis=2)
    up = shifted(pair[:, -HALO:], "rows", 1)
    down = shifted(pair[:, :HALO], "rows", -1)
    return jnp.concatenate([up, pair, down], axis=1)


def divergence(px, py):
    prev_x = jnp.concatenate([jnp.zeros_like(px[:1]), px[:-1]], axis=0)
    prev_y = jnp.concatenate([jnp.zeros_like(py[:, :1]), py[:, :-1]], axis=1)
    return prev_x - px + prev_y - py


def slopes(s):
    down = jnp.concatenate([s[1:] - s[:-1], jnp.zeros_like(s[:1])], axis=0)
    across = jnp.concatenate([s[:, 1:] - s[:, :-1], jnp.zeros_like(s[:, :1])], axis=1)
    return (down, across)


def per_device(video, foreground, scaled_dual):
    rows_here, cols_here, frames = foreground.shape
    total_rows = rows_here * lax.axis_size("rows")
    total_cols = cols_here * lax.axis_size("cols")
    observed = video.astype(jnp.float32)
    mixed = observed - foreground + scaled_dual
    a = observed + scaled_dual
    ext = with_halo(jnp.stack([a, mixed]))
    a_ext, mixed_ext = (ext[0], ext[1])
    flat = mixed.reshape(-1, frames)
    gram = lax.psum(matmul(flat.T, flat), ("rows", "cols"))
    shrink = shrink_matrix(gram)
    ext_rows, ext_cols = (rows_here + 2 * HALO, cols_here + 2 * HALO)
    background_ext = matmul(mixed_ext.reshape(-1, frames), shrink).reshape(
        ext_rows, ext_cols, frames
    )
    target = a_ext - background_ext
    first_row = lax.axis_index("rows") * rows_here - HALO
    first_col = lax.axis_index("cols") * cols_here - HALO
    g = first_row + lax.broadcasted_iota(jnp.int32, (ext_rows, 1, 1), 0)
    h = first_col + lax.broadcasted_iota(jnp.int32, (1, ext_cols, 1), 1)
    keep_x = (g >= 0) & (g <= total_rows - 2)
    keep_y = (h >= 0) & (h <= total_cols - 2)
    dual_x = jnp.zeros_like(target)
    dual_y = jnp.zeros_like(target)
    for sweep in range(K_TV):
        current = target - divergence(dual_x, dual_y)
        down, across = slopes(current)
        dual_x = jnp.where(keep_x, jnp.clip(dual_x + dual_step * down, -tv_weight, tv_weight), 0.0)
        dual_y = jnp.where(
            keep_y, jnp.clip(dual_y + dual_step * across, -tv_weight, tv_weight), 0.0
        )
    inner = (slice(HALO, HALO + rows_here), slice(HALO, HALO + cols_here))
    new_foreground = (target - divergence(dual_x, dual_y))[inner]
    background = background_ext[inner]
    new_dual = target[inner] - new_foreground
    return (background, new_foreground, new_dual)


def solution(mesh):
    return jax.shard_map(
        per_device,
        mesh=mesh,
        in_specs=(P("rows", "cols", None), P("rows", "cols", None), P("rows", "cols", None)),
        out_specs=(P("rows", "cols", None), P("rows", "cols", None), P("rows", "cols", None)),
        check_vma=False,
    )
```

profile of v0, /device:TPU:8, one launch (start us, length us, event | category | flops | bytes accessed | tf_op | source)
XLA Modules:
  0.0 341.0 jit_solution(16815311461451276916)
XLA Ops:
  7.2 5.3 %convolution_bitcast_fusion = f32[256,256]{1,0:T(8,128)} fusion(f32[8,128,256]{2,1,0:T(8,128)} %param.5, f32[8,128,256]{2,1,0:T(8,128)} %param.4, bf16[8,128,256]{2,1,0:T(8,128)(2,1)} %param.3), kind=kOutput, calls=%fused_computation.80 | convolution fusion | flops 806092800 | bytes 2883584 | tf_op jit(solution)/shard_map/dot_general | solution.py:22
  12.5 1.6 fusion.19
  14.2 1.7 collective-permute-start
  15.9 1.5 collective-permute-start.1
  17.4 140.6 %all-reduce.34.cloned.1.call-done = f32[256,256]{1,0:T(8,128)} async-done(((f32[256,256]{1,0:T(8,128)}), f32[256,256]{1,0:T(8,128)}) %all-reduce.34.cloned.1.call-update) | async-done | bytes 262160 | tf_op jit(solution)/shard_map/psum | solution.py:73
  158.1 1.6 multiply_reduce_fusion
  160.4 1.3 fusion.17
  161.9 1.3 fusion.30
  170.6 1.0 select_reduce_fusion
  173.7 5.3 %collective-permute-start.3 = (f32[2,8,144,256]{3,2,1,0:T(8,128)S(1)}, f32[2,8,144,256]{3,2,1,0:T(8,128)S(1)}, u32[]{:S(2)}, u32[]{:S(2)}) collective-permute-start(f32[2,8,144,256]{3,2,1,0:T(8,128)S(1)} %pad_maximum_fusion.1), channel_id=1, source_target_pairs={{2,0},{4,2},{6,4},{8,6},{10,8},{12,10},{14,12},{16,14},{18,16},{20... | collective-permute-start | bytes 7077896 | tf_op jit(solution)/shard_map/ppermute | solution.py:18
  179.0 2.1 collective-permute-start.2
  185.4 44.2 %collective-permute-done.3 = f32[2,8,144,256]{3,2,1,0:T(8,128)S(1)} collective-permute-done((f32[2,8,144,256]{3,2,1,0:T(8,128)S(1)}, f32[2,8,144,256]{3,2,1,0:T(8,128)S(1)}, u32[]{:S(2)}, u32[]{:S(2)}) %collective-permute-start.3) | collective-permute-done | bytes 2359328 | tf_op jit(solution)/shard_map/ppermute | solution.py:18
  229.6 8.3 %collective-permute-done.2 = f32[2,8,144,256]{3,2,1,0:T(8,128)S(1)} collective-permute-done((f32[2,8,144,256]{3,2,1,0:T(8,128)S(1)}, f32[2,8,144,256]{3,2,1,0:T(8,128)S(1)}, u32[]{:S(2)}, u32[]{:S(2)}) %collective-permute-start.2) | collective-permute-done | bytes 2359328 | tf_op jit(solution)/shard_map/ppermute | solution.py:18
  237.9 0.8 pad_maximum_fusion
  238.8 4.9 %fusion = (f32[24,144,256]{2,1,0:T(8,128)S(1)}, f32[24,144,256]{2,1,0:T(8,128)}) fusion(f32[2,24,144,256]{3,2,1,0:T(8,128)S(1)} %pad_maximum_fusion, f32[256,256,1]{1,0,2:T(8,128)S(1)} %fusion.2), kind=kOutput, calls=%fused_computation.10 | convolution fusion | flops 2718793728 | bytes 14417920 | tf_op jit(solution)/shard_map/dot_general | solution.py:22
  245.6 2.1 subtract_subtract_fusion.6
  248.5 2.3 clamp_select_fusion.12
  250.8 2.2 slice.233
  253.7 5.5 %subtract_subtract_fusion.5 = f32[24,144,256]{2,1,0:T(8,128)S(1)} fusion(f32[24,144,256]{2,1,0:T(8,128)S(1)} %get-tuple-element.11, f32[24,144,256]{2,1,0:T(8,128)S(1)} %get-tuple-element.13, f32[24,143,256]{2,1,0:T(8,128)S(1)} %bitcast.98, f32[24,144,256]{2,1,0:T(8,128)} %copy-done.16, f32[23,144,256]{2,1,0:T(8,128)} %slice.233), kind=kLoop, calls=%fused_computation.30 | loop fusion | flops 3538944 | bytes 21061632 | tf_op jit(solution)/shard_map/sub | solution.py:89
  259.9 1.5 copy-done.17
  262.1 1.3 copy-done.5
  263.4 0.7 clamp_select_fusion.10
  264.1 1.1 copy-done.8
  265.2 2.0 slice.239
  267.2 4.9 %subtract_subtract_fusion.4 = f32[24,144,256]{2,1,0:T(8,128)S(1)} fusion(f32[24,144,256]{2,1,0:T(8,128)S(1)} %get-tuple-element.11, f32[24,144,256]{2,1,0:T(8,128)S(1)} %clamp_select_fusion.10, f32[24,143,256]{2,1,0:T(8,128)S(1)} %bitcast.94, f32[24,144,256]{2,1,0:T(8,128)} %copy-done.8, f32[23,144,256]{2,1,0:T(8,128)} %slice.239), kind=kLoop, calls=%fused_computation.27 | loop fusion | flops 3538944 | bytes 21061632 | tf_op jit(solution)/shard_map/sub | solution.py:89
  272.8 1.5 copy-done.9
  275.0 2.9 clamp_select_fusion.8
  278.0 2.0 slice.245
  280.0 1.2 copy-done
  281.2 4.9 %subtract_subtract_fusion.3 = f32[24,144,256]{2,1,0:T(8,128)S(1)} fusion(f32[24,144,256]{2,1,0:T(8,128)S(1)} %get-tuple-element.11, f32[24,144,256]{2,1,0:T(8,128)S(1)} %copy-done, f32[24,143,256]{2,1,0:T(8,128)S(1)} %bitcast.95, f32[24,144,256]{2,1,0:T(8,128)} %copy-done.10, f32[23,144,256]{2,1,0:T(8,128)} %slice.245), kind=kLoop, calls=%fused_computation.24 | loop fusion | flops 3538944 | bytes 21061632 | tf_op jit(solution)/shard_map/sub | solution.py:89
  286.8 1.5 copy-done.11
  288.3 0.8 clamp_select_fusion.7
  289.2 2.9 clamp_select_fusion.6
  292.1 2.0 slice.251
  294.1 1.2 copy-done.1
  295.3 4.9 %subtract_subtract_fusion.2 = f32[24,144,256]{2,1,0:T(8,128)S(1)} fusion(f32[24,144,256]{2,1,0:T(8,128)S(1)} %get-tuple-element.11, f32[24,144,256]{2,1,0:T(8,128)S(1)} %copy-done.1, f32[24,143,256]{2,1,0:T(8,128)S(1)} %bitcast.96, f32[24,144,256]{2,1,0:T(8,128)} %copy-done.12, f32[23,144,256]{2,1,0:T(8,128)} %slice.251), kind=kLoop, calls=%fused_computation.21 | loop fusion | flops 3538944 | bytes 21061632 | tf_op jit(solution)/shard_map/sub | solution.py:89
  301.0 1.5 copy-done.13
  303.2 3.0 clamp_select_fusion.4
  306.2 2.0 slice.257
  308.2 1.2 copy-done.2
  309.4 4.9 %subtract_subtract_fusion.1 = f32[24,144,256]{2,1,0:T(8,128)S(1)} fusion(f32[24,144,256]{2,1,0:T(8,128)S(1)} %get-tuple-element.11, f32[24,144,256]{2,1,0:T(8,128)S(1)} %copy-done.2, f32[24,143,256]{2,1,0:T(8,128)S(1)} %bitcast.97, f32[24,144,256]{2,1,0:T(8,128)} %copy-done.14, f32[23,144,256]{2,1,0:T(8,128)} %slice.257), kind=kLoop, calls=%fused_computation.18 | loop fusion | flops 3538944 | bytes 21061632 | tf_op jit(solution)/shard_map/sub | solution.py:89
  315.1 1.5 copy-done.15
  317.3 1.3 copy-done.3
  319.3 1.1 copy-done.6
  320.4 2.0 slice.263
  322.4 4.9 %subtract_subtract_fusion = f32[24,144,256]{2,1,0:T(8,128)S(1)} fusion(f32[24,144,256]{2,1,0:T(8,128)S(1)} %get-tuple-element.11, f32[24,144,256]{2,1,0:T(8,128)S(1)} %clamp_select_fusion.2, f32[24,143,256]{2,1,0:T(8,128)S(1)} %bitcast.93, f32[24,144,256]{2,1,0:T(8,128)} %copy-done.6, f32[23,144,256]{2,1,0:T(8,128)} %slice.263), kind=kLoop, calls=%fused_computation.15 | loop fusion | flops 3538944 | bytes 21061632 | tf_op jit(solution)/shard_map/sub | solution.py:89
  328.0 2.5 slice.223
  332.2 1.8 slice_subtract_fusion.18
  (95 shorter events, 25.8 us)
Async XLA Ops:
  7.2 5.4 %copy-start.18 = (f32[8,128,256]{2,1,0:T(8,128)S(1)}, f32[8,128,256]{2,1,0:T(8,128)}, u32[]{:S(2)}) copy-start(f32[8,128,256]{2,1,0:T(8,128)} %param.5) | copy-start | bytes 3145732
  7.2 150.9 %all-reduce.34.cloned.1.call-start = ((), (), s32[]{:S(2)}) async-start(), calls=%async_computation | async-start | bytes 524288 | tf_op jit(solution)/shard_map/psum | solution.py:73
  14.2 159.3 %collective-permute-start = (f32[2,8,8,256]{3,2,1,0:T(8,128)S(1)}, f32[2,8,8,256]{3,2,1,0:T(8,128)S(1)}, u32[]{:S(2)}, u32[]{:S(2)}) collective-permute-start(f32[2,8,8,256]{3,2,1,0:T(8,128)S(1)} %get-tuple-element.5), channel_id=1, source_target_pairs={{0,1},{2,3},{4,5},{6,7},{8,9},{10,11},{12,13},{14,15},{16,17},{18,... | collective-permute-start | bytes 393224 | tf_op jit(solution)/shard_map/ppermute | solution.py:18
  15.9 157.6 %collective-permute-start.1 = (f32[2,8,8,256]{3,2,1,0:T(8,128)S(1)}, f32[2,8,8,256]{3,2,1,0:T(8,128)S(1)}, u32[]{:S(2)}, u32[]{:S(2)}) collective-permute-start(f32[2,8,8,256]{3,2,1,0:T(8,128)S(1)} %get-tuple-element.6), channel_id=1, source_target_pairs={{1,0},{3,2},{5,4},{7,6},{9,8},{11,10},{13,12},{15,14},{17,16},{19,... | collective-permute-start | bytes 393224 | tf_op jit(solution)/shard_map/ppermute | solution.py:18
  173.7 55.9 %collective-permute-start.3 = (f32[2,8,144,256]{3,2,1,0:T(8,128)S(1)}, f32[2,8,144,256]{3,2,1,0:T(8,128)S(1)}, u32[]{:S(2)}, u32[]{:S(2)}) collective-permute-start(f32[2,8,144,256]{3,2,1,0:T(8,128)S(1)} %pad_maximum_fusion.1), channel_id=1, source_target_pairs={{2,0},{4,2},{6,4},{8,6},{10,8},{12,10},{14,12},{16,14},{18,16},{20... | collective-permute-start | bytes 7077896 | tf_op jit(solution)/shard_map/ppermute | solution.py:18
  179.0 58.9 %collective-permute-start.2 = (f32[2,8,144,256]{3,2,1,0:T(8,128)S(1)}, f32[2,8,144,256]{3,2,1,0:T(8,128)S(1)}, u32[]{:S(2)}, u32[]{:S(2)}) collective-permute-start(f32[2,8,144,256]{3,2,1,0:T(8,128)S(1)} %pad_maximum_fusion.1), channel_id=1, source_target_pairs={{0,2},{2,4},{4,6},{6,8},{8,10},{10,12},{12,14},{14,16},{16,18},{18... | collective-permute-start | bytes 7077896 | tf_op jit(solution)/shard_map/ppermute | solution.py:18
  250.8 2.9 copy-start.16
  250.8 8.3 %copy-start.4 = (f32[24,144,256]{2,1,0:T(8,128)}, f32[24,144,256]{2,1,0:T(8,128)S(1)}, u32[]{:S(2)}) copy-start(f32[24,144,256]{2,1,0:T(8,128)S(1)} %get-tuple-element.13) | copy-start | bytes 10616836
  259.4 2.0 copy-start.17
  261.4 2.0 copy-start.5
  263.4 1.8 copy-start.8
  272.3 2.0 copy-start.9
  275.0 2.9 copy-start.10
  278.0 3.2 copy-start
  286.3 2.0 copy-start.11
  289.2 2.9 copy-start.12
  292.1 3.2 copy-start.1
  300.5 2.0 copy-start.13
  303.2 3.0 copy-start.14
  306.2 3.2 copy-start.2
  314.6 2.0 copy-start.15
  316.6 2.0 copy-start.3
  318.6 1.8 copy-start.6
  327.6 3.0 copy-start.7
Sparse Core Ops, SparseCore 0:
  13.3 144.7 all-reduce.33
where the time goes:
time: 344 us; the launch traced here: 341 us
  waiting for transfers between devices  193 us (56%)
  other arithmetic  62.3 us (18%)
  local copies, waits for them, and re-layouts  31.9 us (9%)
  matrix products  26.6 us (8%)
  between operations  16.3 us (5%)
  starting transfers between devices  10.7 us (3%)
    psum x1, waiting for transfers between devices, per_device(): gram = lax.psum(matmul(flat.T, flat), ('rows', 'cols'))  141 us
    ppermute x4, waiting for transfers between devices, shifted(): return lax.ppermute(x, axis, pairs)  52.5 us
    sub x7, other arithmetic, per_device(): current = target - divergence(dual_x, dual_y)  32.1 us
    dot_general x39, matrix products, matmul(): jnp.dot(left, right, precision=lax.Precision.HIGHEST, preferred_element_t...  26.6 us
    unnamed x38, local copies, waits for them, and re-layouts  16.6 us
    select_n x8, other arithmetic, per_device(): jnp.where(keep_y, jnp.clip(dual_y + dual_step * across, -tv_weight, tv_we...  13.8 us
    slice x8, local copies, waits for them, and re-layouts, divergence(): prev_x = jnp.concatenate([jnp.zeros_like(px[:1]), px[:-1]], axis=0)  12.7 us
    ppermute x4, starting transfers between devices, shifted(): return lax.ppermute(x, axis, pairs)  10.6 us
  transfers between devices with their start and end apart: 5, of which 3 were waited for; matrix products, arithmetic and copies ran while one was open for 6% of the time, Pallas kernels for 0%

commit v1 on v0

--- a/solution.py
+++ b/solution.py
@@ -70,7 +70,9 @@
     ext = with_halo(jnp.stack([a, mixed]))
     a_ext, mixed_ext = (ext[0], ext[1])
     flat = mixed.reshape(-1, frames)
-    gram = lax.psum(matmul(flat.T, flat), ("rows", "cols"))
+    own = matmul(flat.T, flat)
+    parts = lax.all_gather(own, ("rows", "cols"), axis=0, tiled=False)
+    gram = parts.sum(axis=0)
     shrink = shrink_matrix(gram)
     ext_rows, ext_cols = (rows_here + 2 * HALO, cols_here + 2 * HALO)
     background_ext = matmul(mixed_ext.reshape(-1, frames), shrink).reshape(

time: 344 us -> 296 us (0.86)
  waiting for transfers between devices: 193 us -> 132 us
  other arithmetic: 62.3 us -> 74.2 us
    psum x1 -> x0, waiting for transfers between devices: 141 us -> none  [per_device(): gram = lax.psum(matmul(flat.T, flat), ('rows', 'cols'))]
    all_gather x0 -> x1, waiting for transfers between devices: none -> 77.7 us  [per_device(): parts = lax.all_gather(own, ('rows', 'cols'), axis=0, tiled=False)]
    reduce_sum x0 -> x1, other arithmetic: none -> 12.1 us  [per_device(): gram = parts.sum(axis=0)]
    select_n x8, other arithmetic: 13.8 us -> 8.8 us  [per_device(): jnp.where(keep_y, jnp.clip(dual_y + dual_step * across, -tv_weight, tv_we...]
    concatenate x1, other arithmetic: 0.8 us -> 4.87 us  [with_halo(): return jnp.concatenate([up, pair, down], axis=1)]
    unnamed x38 -> x30, local copies, waits for them, and re-layouts: 16.6 us -> 14.3 us
  transfers between devices with their start and end apart: 5 -> 5, of which waited for: 3 -> 3; matrix products, arithmetic and copies ran while one was open for 6% -> 3% of each run, Pallas kernels for 0% -> 0%
where the time goes in v1:
time: 296 us; the launch traced here: 291 us
  waiting for transfers between devices  132 us (45%)
  other arithmetic  74.2 us (25%)
  local copies, waits for them, and re-layouts  29.5 us (10%)
  matrix products  25.6 us (9%)
  between operations  16.4 us (6%)
  starting transfers between devices  13.1 us (4%)
    all_gather x1, waiting for transfers between devices, per_device(): parts = lax.all_gather(own, ('rows', 'cols'), axis=0, tiled=False)  77.7 us
    ppermute x4, waiting for transfers between devices, shifted(): return lax.ppermute(x, axis, pairs)  54.6 us
    sub x7, other arithmetic, per_device(): current = target - divergence(dual_x, dual_y)  32.4 us
    dot_general x39, matrix products, matmul(): jnp.dot(left, right, precision=lax.Precision.HIGHEST, preferred_element_t...  25.6 us
    unnamed x30, local copies, waits for them, and re-layouts  14.3 us
    ppermute x4, starting transfers between devices, shifted(): return lax.ppermute(x, axis, pairs)  13.1 us
    slice x8, local copies, waits for them, and re-layouts, divergence(): prev_x = jnp.concatenate([jnp.zeros_like(px[:1]), px[:-1]], axis=0)  12.9 us
    reduce_sum x1, other arithmetic, per_device(): gram = parts.sum(axis=0)  12.1 us
  transfers between devices with their start and end apart: 5, of which 3 were waited for; matrix products, arithmetic and copies ran while one was open for 3% of the time, Pallas kernels for 0%

profile of v1, /device:TPU:8, one launch (start us, length us, event | category | flops | bytes accessed | tf_op | source)
XLA Modules:
  0.0 291.1 jit_solution(12433850203861000537)
XLA Ops:
  7.2 5.2 %convolution_bitcast_fusion = f32[256,256]{1,0:T(8,128)} fusion(f32[8,128,256]{2,1,0:T(8,128)} %param.5, f32[8,128,256]{2,1,0:T(8,128)} %param.4, bf16[8,128,256]{2,1,0:T(8,128)(2,1)} %param.3), kind=kOutput, calls=%fused_computation.80 | convolution fusion | flops 806092800 | bytes 2883584 | tf_op jit(solution)/shard_map/dot_general | solution.py:22
  12.4 1.6 fusion.19
  14.0 1.7 collective-permute-start
  15.8 1.3 collective-permute-start.1
  17.1 1.9 collective-permute-done.1
  19.0 1.6 pad_maximum_fusion.1
  20.6 3.4 %collective-permute-start.2 = (f32[2,8,144,256]{3,2,1,0:T(8,128)}, f32[2,8,144,256]{3,2,1,0:T(8,128)}, u32[]{:S(2)}, u32[]{:S(2)}) collective-permute-start(f32[2,8,144,256]{3,2,1,0:T(8,128)} %pad_maximum_fusion.1), channel_id=1, source_target_pairs={{0,2},{2,4},{4,6},{6,8},{8,10},{10,12},{12,14},{14,16},{16,18},{18... | collective-permute-start | bytes 7077896 | tf_op jit(solution)/shard_map/ppermute | solution.py:18
  24.0 6.7 %collective-permute-start.3 = (f32[2,8,144,256]{3,2,1,0:T(8,128)}, f32[2,8,144,256]{3,2,1,0:T(8,128)}, u32[]{:S(2)}, u32[]{:S(2)}) collective-permute-start(f32[2,8,144,256]{3,2,1,0:T(8,128)} %pad_maximum_fusion.1), channel_id=1, source_target_pairs={{2,0},{4,2},{6,4},{8,6},{10,8},{12,10},{14,12},{16,14},{18,16},{20... | collective-permute-start | bytes 7077896 | tf_op jit(solution)/shard_map/ppermute | solution.py:18
  30.7 52.6 %collective-permute-done.2 = f32[2,8,144,256]{3,2,1,0:T(8,128)} collective-permute-done((f32[2,8,144,256]{3,2,1,0:T(8,128)}, f32[2,8,144,256]{3,2,1,0:T(8,128)}, u32[]{:S(2)}, u32[]{:S(2)}) %collective-permute-start.2) | collective-permute-done | bytes 2359328 | tf_op jit(solution)/shard_map/ppermute | solution.py:18
  83.4 4.9 %pad_maximum_fusion = f32[2,24,144,256]{3,2,1,0:T(8,128)} fusion(f32[2,8,144,256]{3,2,1,0:T(8,128)} %collective-permute-done.3, f32[2,8,8,256]{3,2,1,0:T(8,128)S(1)} %collective-permute-done.1, f32[1,8,128,256]{3,2,1,0:T(8,128)S(1)} %get-tuple-element.8, f32[1,8,128,256]{3,2,1,0:T(8,128)S(1)} %get-tuple-element.7, ...), kind=kLoop, calls=%fused_computation | loop fusion | flops 8847360 | bytes 14155776 | tf_op jit(solution)/shard_map/concatenate | solution.py:48
  88.2 77.7 %all-gather.3.cloned.1.call-done = f32[32768,256]{1,0:T(8,128)} async-done(((f32[256,256]{1,0:T(8,128)}), f32[32768,256]{1,0:T(8,128)}) %all-gather.3.cloned.1.call-update) | async-done | bytes 33554448 | tf_op jit(solution)/shard_map/all_gather | solution.py:74
  166.0 12.1 %reduce_sum.28 = f32[256,256]{1,0:T(8,128)S(1)} reduce(f32[128,256,256]{2,1,0:T(8,128)} %bitcast.100, f32[]{:T(128)} %constant.16.clone.1), dimensions={0}, to_apply=%region_0.0 | reduce | flops 8323072 | bytes 33816580 | tf_op jit(solution)/shard_map/reduce_sum | solution.py:75
  187.9 1.0 select_reduce_fusion
  189.5 1.3 fusion.9
  196.2 4.7 %fusion = (f32[24,144,256]{2,1,0:T(8,128)S(1)}, f32[24,144,256]{2,1,0:T(8,128)}) fusion(f32[2,24,144,256]{3,2,1,0:T(8,128)S(1)} %bitcast.103, f32[256,256,1]{1,0,2:T(8,128)S(1)} %fusion.2), kind=kOutput, calls=%fused_computation.10 | convolution fusion | flops 2718793728 | bytes 14417920 | tf_op jit(solution)/shard_map/dot_general | solution.py:22
  202.9 2.1 subtract_subtract_fusion.6
  205.8 2.2 clamp_select_fusion.12
  208.0 2.2 slice.233
  210.9 4.9 %subtract_subtract_fusion.5 = f32[24,144,256]{2,1,0:T(8,128)S(1)} fusion(f32[24,144,256]{2,1,0:T(8,128)S(1)} %get-tuple-element.11, f32[24,144,256]{2,1,0:T(8,128)S(1)} %get-tuple-element.13, f32[24,143,256]{2,1,0:T(8,128)S(1)} %bitcast.99, f32[24,144,256]{2,1,0:T(8,128)} %copy-done.9, f32[23,144,256]{2,1,0:T(8,128)} %slice.233), kind=kLoop, calls=%fused_computation.30 | loop fusion | flops 3538944 | bytes 21061632 | tf_op jit(solution)/shard_map/sub | solution.py:91
  216.5 1.5 copy-done.10
  218.0 0.7 clamp_select_fusion.11
  218.7 2.2 slice.239
  220.9 0.7 clamp_select_fusion.10
  221.6 4.9 %subtract_subtract_fusion.4 = f32[24,144,256]{2,1,0:T(8,128)S(1)} fusion(f32[24,144,256]{2,1,0:T(8,128)S(1)} %get-tuple-element.11, f32[24,144,256]{2,1,0:T(8,128)S(1)} %clamp_select_fusion.10, f32[24,143,256]{2,1,0:T(8,128)S(1)} %bitcast.95, f32[24,144,256]{2,1,0:T(8,128)} %copy-done.3, f32[23,144,256]{2,1,0:T(8,128)} %slice.239), kind=kLoop, calls=%fused_computation.27 | loop fusion | flops 3538944 | bytes 21061632 | tf_op jit(solution)/shard_map/sub | solution.py:91
  227.3 1.5 copy-done.4
  229.5 1.8 copy-done.5
  231.3 2.0 slice.245
  233.3 0.7 clamp_select_fusion.8
  234.0 4.9 %subtract_subtract_fusion.3 = f32[24,144,256]{2,1,0:T(8,128)S(1)} fusion(f32[24,144,256]{2,1,0:T(8,128)S(1)} %get-tuple-element.11, f32[24,144,256]{2,1,0:T(8,128)S(1)} %clamp_select_fusion.8, f32[24,143,256]{2,1,0:T(8,128)S(1)} %bitcast.96, f32[24,144,256]{2,1,0:T(8,128)} %copy-done.5, f32[23,144,256]{2,1,0:T(8,128)} %slice.245), kind=kLoop, calls=%fused_computation.24 | loop fusion | flops 3538944 | bytes 21061632 | tf_op jit(solution)/shard_map/sub | solution.py:91
  239.6 1.5 copy-done.6
  241.2 0.8 clamp_select_fusion.7
  242.0 2.0 slice.251
  244.0 2.5 clamp_select_fusion.6
  246.5 5.8 %subtract_subtract_fusion.2 = f32[24,144,256]{2,1,0:T(8,128)S(1)} fusion(f32[24,144,256]{2,1,0:T(8,128)S(1)} %get-tuple-element.11, f32[24,144,256]{2,1,0:T(8,128)} %clamp_select_fusion.6, f32[24,143,256]{2,1,0:T(8,128)} %bitcast.97, f32[24,144,256]{2,1,0:T(8,128)S(1)} %clamp_select_fusion.7, f32[23,144,256]{2,1,0:T(8,128)} %slice.251), kind=kLoop, calls=%fused_computation.21 | loop fusion | flops 3538944 | bytes 21061632 | tf_op jit(solution)/shard_map/sub | solution.py:91
  253.0 0.7 clamp_select_fusion.5
  253.7 2.0 slice.257
  255.8 2.5 copy-done
  258.2 0.7 clamp_select_fusion.4
  258.9 4.9 %subtract_subtract_fusion.1 = f32[24,144,256]{2,1,0:T(8,128)S(1)} fusion(f32[24,144,256]{2,1,0:T(8,128)S(1)} %get-tuple-element.11, f32[24,144,256]{2,1,0:T(8,128)S(1)} %clamp_select_fusion.4, f32[24,143,256]{2,1,0:T(8,128)S(1)} %bitcast.98, f32[24,144,256]{2,1,0:T(8,128)} %copy-done.7, f32[23,144,256]{2,1,0:T(8,128)} %slice.257), kind=kLoop, calls=%fused_computation.18 | loop fusion | flops 3538944 | bytes 21061632 | tf_op jit(solution)/shard_map/sub | solution.py:91
  264.6 1.5 copy-done.8
  266.8 1.8 copy-done.1
  268.6 2.0 slice.263
  270.6 0.7 clamp_select_fusion.2
  271.3 4.9 %subtract_subtract_fusion = f32[24,144,256]{2,1,0:T(8,128)S(1)} fusion(f32[24,144,256]{2,1,0:T(8,128)S(1)} %get-tuple-element.11, f32[24,144,256]{2,1,0:T(8,128)S(1)} %clamp_select_fusion.2, f32[24,143,256]{2,1,0:T(8,128)S(1)} %bitcast.94, f32[24,144,256]{2,1,0:T(8,128)} %copy-done.1, f32[23,144,256]{2,1,0:T(8,128)} %slice.263), kind=kLoop, calls=%fused_computation.15 | loop fusion | flops 3538944 | bytes 21061632 | tf_op jit(solution)/shard_map/sub | solution.py:91
  277.0 1.5 copy-done.2
  279.4 0.7 clamp_select_fusion
  280.1 2.3 slice.223
  282.4 1.7 slice_subtract_fusion.18
  (89 shorter events, 24.1 us)
Async XLA Ops:
  7.2 5.2 %copy-start.11 = (f32[8,128,256]{2,1,0:T(8,128)S(1)}, f32[8,128,256]{2,1,0:T(8,128)}, u32[]{:S(2)}) copy-start(f32[8,128,256]{2,1,0:T(8,128)} %param.5) | copy-start | bytes 3145732
  7.2 158.8 %all-gather.3.cloned.1.call-start = ((), (), s32[]{:S(2)}) async-start(), calls=%async_computation | async-start | bytes 33816576 | tf_op jit(solution)/shard_map/all_gather | solution.py:74
  14.0 3.1 %collective-permute-start = (f32[2,8,8,256]{3,2,1,0:T(8,128)S(1)}, f32[2,8,8,256]{3,2,1,0:T(8,128)S(1)}, u32[]{:S(2)}, u32[]{:S(2)}) collective-permute-start(f32[2,8,8,256]{3,2,1,0:T(8,128)S(1)} %get-tuple-element.5), channel_id=1, source_target_pairs={{0,1},{2,3},{4,5},{6,7},{8,9},{10,11},{12,13},{14,15},{16,17},{18,... | collective-permute-start | bytes 393224 | tf_op jit(solution)/shard_map/ppermute | solution.py:18
  15.8 3.2 %collective-permute-start.1 = (f32[2,8,8,256]{3,2,1,0:T(8,128)S(1)}, f32[2,8,8,256]{3,2,1,0:T(8,128)S(1)}, u32[]{:S(2)}, u32[]{:S(2)}) collective-permute-start(f32[2,8,8,256]{3,2,1,0:T(8,128)S(1)} %get-tuple-element.6), channel_id=1, source_target_pairs={{1,0},{3,2},{5,4},{7,6},{9,8},{11,10},{13,12},{15,14},{17,16},{19,... | collective-permute-start | bytes 393224 | tf_op jit(solution)/shard_map/ppermute | solution.py:18
  20.6 62.7 %collective-permute-start.2 = (f32[2,8,144,256]{3,2,1,0:T(8,128)}, f32[2,8,144,256]{3,2,1,0:T(8,128)}, u32[]{:S(2)}, u32[]{:S(2)}) collective-permute-start(f32[2,8,144,256]{3,2,1,0:T(8,128)} %pad_maximum_fusion.1), channel_id=1, source_target_pairs={{0,2},{2,4},{4,6},{6,8},{8,10},{10,12},{12,14},{14,16},{16,18},{18... | collective-permute-start | bytes 7077896 | tf_op jit(solution)/shard_map/ppermute | solution.py:18
  24.0 59.3 %collective-permute-start.3 = (f32[2,8,144,256]{3,2,1,0:T(8,128)}, f32[2,8,144,256]{3,2,1,0:T(8,128)}, u32[]{:S(2)}, u32[]{:S(2)}) collective-permute-start(f32[2,8,144,256]{3,2,1,0:T(8,128)} %pad_maximum_fusion.1), channel_id=1, source_target_pairs={{2,0},{4,2},{6,4},{8,6},{10,8},{12,10},{14,12},{16,14},{18,16},{20... | collective-permute-start | bytes 7077896 | tf_op jit(solution)/shard_map/ppermute | solution.py:18
  186.3 9.9 %slice-start = ((s8[7077888]{0:T(1024)(128)(4,1)}), s8[2883584]{0:T(1024)(128)(4,1)S(1)}, s32[]{:S(2)}) async-start(s8[7077888]{0:T(1024)(128)(4,1)} %bitcast.102), calls=%async_computation.1 | async-start | bytes 5767168
  187.8 1.0 copy-start.12
  192.0 4.1 %slice-start.1 = ((s8[7077888]{0:T(1024)(128)(4,1)}), s8[4194304]{0:T(1024)(128)(4,1)S(1)}, s32[]{:S(2)}) async-start(s8[7077888]{0:T(1024)(128)(4,1)} %bitcast.102), calls=%async_computation.2 | async-start | bytes 8388608
  208.0 2.9 copy-start.9
  216.0 2.0 copy-start.10
  218.7 2.9 copy-start.3
  226.8 2.0 copy-start.4
  229.5 1.8 copy-start.5
  239.1 2.0 copy-start.6
  253.7 5.2 %copy-start.7 = (f32[24,144,256]{2,1,0:T(8,128)}, f32[24,144,256]{2,1,0:T(8,128)S(1)}, u32[]{:S(2)}) copy-start(f32[24,144,256]{2,1,0:T(8,128)S(1)} %clamp_select_fusion.5) | copy-start | bytes 10616836
  253.7 4.5 %copy-start = (f32[24,144,256]{2,1,0:T(8,128)S(1)}, f32[24,144,256]{2,1,0:T(8,128)}, u32[]{:S(2)}) copy-start(f32[24,144,256]{2,1,0:T(8,128)} %clamp_select_fusion.6) | copy-start | bytes 10616836
  264.1 2.0 copy-start.8
  266.8 1.8 copy-start.1
  276.5 2.0 copy-start.2
Sparse Core Ops, SparseCore 0:
  12.5 153.3 all-gather.2
